TPU v7x, 256 devices: a whole 4x4x8 slice. The times are simulated.
256 devices in a mesh: seq: 32 (over z, y), mp: 4 (over x), req: 2 (over core).
Axes of the slice: x: 4, y: 4, z: 8, core: 2. Of those that a mesh axis runs over, the one named last changes fastest.
Arguments:
- hidden: bfloat16 [2, 8192, 3072], P('req', 'seq', 'mp'), may hold values from -6 to 6
- norm_gain: bfloat16 [3072], replicated, may hold values from 0.5 to 1.5
- w_query: bfloat16 [3072, 1024], P(None, 'mp'), may hold values from -0.109375 to 0.109375
- w_keyval: bfloat16 [3072, 512], P(None, 'mp'), may hold values from -0.109375 to 0.109375
- w_attn_out: bfloat16 [1024, 3072], P('mp'), may hold values from -1.5 to 1.5
- w_inner: bfloat16 [3072, 2, 1536], P(None, None, 'mp'), may hold values from -0.109375 to 0.109375
- w_bc: bfloat16 [3072, 512], P(None, 'mp'), may hold values from -0.109375 to 0.109375
- w_dt: bfloat16 [3072, 12], P(None, 'mp'), may hold values from -0.109375 to 0.109375
- dt_bias: float32 [12], P('mp'), may hold values from -4 to 0
- a_log: float32 [12], P('mp'), may hold values from -12 to 0
- d_skip: float32 [12], P('mp'), may hold values from 0.1 to 10
- conv_x: bfloat16 [4, 1536], P(None, 'mp'), may hold values from -3 to 3
- conv_bc: bfloat16 [4, 512], replicated, may hold values from -3 to 3
- mamba_gain: bfloat16 [1536], P('mp'), may hold values from 0.5 to 1.5
- w_mamba_out: bfloat16 [1536, 3072], P('mp'), may hold values from -0.15625 to 0.15625
- cache: bfloat16 [2, 8192, 512], P('req', 'seq', 'mp'), may hold values from -70 to 70, as said below
- cache_len: int32 [2], P('req'), may hold values from 256 to 8192
- tail_x: bfloat16 [2, 3, 1536], P('req', None, 'mp'), may hold values from -6 to 6
- tail_bc: bfloat16 [2, 3, 512], P('req'), may hold values from -6 to 6
- ssm_init: float32 [2, 12, 128, 256], P('req', 'mp'), may hold values from -6 to 6
Outputs:
- layer_out: bfloat16 [2, 8192, 3072], P('req', 'seq', 'mp')
- new_keyval: bfloat16 [2, 8192, 512], P('req', 'seq', 'mp')
- block_states: float32 [2, 32, 12, 128, 256], P('req', 'seq', 'mp')
Inputs may be any that keep to these rules, and one draw needn't show every extreme that they name: Rows of the cache at or past cache_len are unused.
All inputs are finite; a program needn't handle non-finite values.
Results may differ from a plain program's by a relative error of at most 0.0097.
Values may be sent and summed in bfloat16 or wider, within the bound.
A program may use at most 192 MiB of HBM per device.

v0:
```python
import jax
import jax.numpy as jnp
from jax import lax
from jax.sharding import PartitionSpec as P

HD = 128
QH = 8
KVH = 2
NS = 256
CONV = 4
epsilon = 1e-05
rope_base = 100000000000.0
negative = -1e30


def shifted(block, axis, distance):
    devices = range(lax.axis_size(axis))
    route = [(i - distance, i) for i in devices if i - distance in devices]
    return lax.ppermute(block, axis, route)


def prefix(part, axis, combine, identity):
    place = lax.axis_index(axis)
    gathered = jax.tree.map(lambda a: lax.all_gather(a, axis), part)
    state = jax.tree.map(lambda a, e: jnp.zeros_like(a) + jnp.asarray(e, a.dtype), part, identity)

    def one(turn, state):
        return combine(
            state, jax.tree.map(lambda a: lax.dynamic_index_in_dim(a, turn, 0, False), gathered)
        )

    return lax.fori_loop(0, place, one, state)


def rotate(values, positions):
    half = HD // 2
    freqs = rope_base ** (-jnp.arange(half, dtype=jnp.float32) * 2.0 / HD)
    angles = positions.astype(jnp.float32)[:, None] * freqs[None, :]
    cosine = jnp.cos(angles)[:, None, :]
    sine = jnp.sin(angles)[:, None, :]
    first = values[..., :half]
    second = values[..., half:]
    return jnp.concatenate(
        [first * cosine - second * sine, second * cosine + first * sine], axis=-1
    )


def rms_scale(values):
    mean_sq = jnp.mean(values * values, axis=-1, keepdims=True)
    return values * lax.rsqrt(mean_sq + epsilon)


def causal_conv(tail, inputs, taps):
    padded = jnp.concatenate([tail, inputs], axis=0).astype(jnp.float32)
    count = inputs.shape[0]
    total = jnp.zeros(inputs.shape, jnp.float32)
    for offset in range(CONV):
        total = total + taps[offset].astype(jnp.float32)[None, :] * padded[offset : offset + count]
    return jax.nn.silu(total)


def join_states(earlier, later):
    return (earlier[0] * later[0], later[0][:, None, None] * earlier[1] + later[1])


def shards(
    hidden,
    norm_gain,
    w_query,
    w_keyval,
    w_attn_out,
    w_inner,
    w_bc,
    w_dt,
    dt_bias,
    a_log,
    d_skip,
    conv_x,
    conv_bc,
    mamba_gain,
    w_mamba_out,
    cache,
    cache_len,
    tail_x,
    tail_bc,
    ssm_init,
):
    high = lax.Precision.HIGHEST
    own_rows = hidden[0]
    tokens = own_rows.shape[0]
    seq_pos = lax.axis_index("seq")
    mp_pos = lax.axis_index("mp")
    length = cache_len[0]
    whole = lax.all_gather(own_rows, "mp", axis=1, tiled=True)
    normed = (rms_scale(whole.astype(jnp.float32)) * norm_gain.astype(jnp.float32)).astype(
        jnp.bfloat16
    )
    positions = length + seq_pos * tokens + jnp.arange(tokens, dtype=jnp.int32)
    local_heads = w_query.shape[1] // HD
    query = rotate(
        jnp.dot(normed, w_query, preferred_element_type=jnp.float32).reshape(
            tokens, local_heads, HD
        ),
        positions,
    ).astype(jnp.bfloat16)
    projected = jnp.dot(normed, w_keyval, preferred_element_type=jnp.float32)
    roped = rotate(projected[:, None, :], positions)[:, 0, :]
    kv_block = jnp.where(mp_pos % 2 == 0, roped, projected).astype(jnp.bfloat16)
    bc_block = jnp.dot(normed, w_bc, preferred_element_type=jnp.float32).astype(jnp.bfloat16)
    bc_all = lax.all_gather(bc_block, "mp", axis=1, tiled=True)
    mp_size = lax.axis_size("mp")
    pairs_of = [(i, i ^ 1) for i in range(mp_size)]
    is_key_block = mp_pos % 2 == 0

    def paired(own):
        other = lax.ppermute(own, "mp", pairs_of)
        return jnp.where(
            is_key_block,
            jnp.concatenate([own, other], axis=1),
            jnp.concatenate([other, own], axis=1),
        )

    cache_all = lax.all_gather(paired(cache[0]), "seq", axis=0, tiled=True)
    new_all = lax.all_gather(paired(kv_block), "seq", axis=0, tiled=True)
    inner = jnp.einsum("td,dkc->tkc", normed, w_inner, preferred_element_type=jnp.float32).astype(
        jnp.bfloat16
    )
    rim = CONV - 1
    prev_x, prev_bc = shifted((inner[tokens - rim :, 1], bc_all[tokens - rim :]), "seq", 1)
    first_block = seq_pos == 0
    prev_x = jnp.where(first_block, tail_x[0], prev_x)
    prev_bc = jnp.where(first_block, tail_bc[0], prev_bc)
    mamba_heads = dt_bias.shape[0]
    x_conv = causal_conv(prev_x, inner[:, 1], conv_x).reshape(tokens, mamba_heads, HD)
    bc_conv = causal_conv(prev_bc, bc_all, conv_bc)
    b_mat = bc_conv[:, :NS]
    c_mat = bc_conv[:, NS:]
    step_size = jax.nn.softplus(jnp.dot(normed, w_dt, preferred_element_type=jnp.float32) + dt_bias)
    log_decay = -step_size * jnp.exp(a_log)[None, :]
    cumulative = jnp.cumsum(log_decay, axis=0)
    pairs = jnp.dot(c_mat, b_mat.T, precision=high)
    gap = cumulative[:, None, :] - cumulative[None, :, :]
    token_ids = jnp.arange(tokens)
    lower = (token_ids[:, None] >= token_ids[None, :])[:, :, None]
    decay = jnp.where(lower, jnp.exp(jnp.where(lower, gap, 0.0)), 0.0)
    mixing = decay * pairs[:, :, None] * step_size[None, :, :]
    inner_out = jnp.einsum("tsh,shp->thp", mixing, x_conv, precision=high)
    to_end = jnp.exp(cumulative[-1][None, :] - cumulative) * step_size
    own_state = jnp.einsum("sh,shp,sn->hpn", to_end, x_conv, b_mat, precision=high)
    block_decay = jnp.exp(cumulative[-1])
    seq_size = lax.axis_size("seq")
    rows = HD // seq_size
    pieces = jnp.transpose(own_state.reshape(mamba_heads, seq_size, rows, NS), (1, 0, 2, 3))
    decays = jnp.broadcast_to(block_decay[None, :, None, None], (seq_size, mamba_heads, 1, NS))
    columns = lax.all_to_all(jnp.concatenate([pieces, decays], axis=2), "seq", 0, 0, tiled=True)
    carry = lax.dynamic_slice_in_dim(ssm_init[0], seq_pos * rows, rows, 1)
    entering = []
    for source in range(seq_size):
        entering.append(carry)
        part = columns[source]
        carry = part[:, rows:, :] * carry + part[:, :rows, :]
    entering = lax.all_to_all(jnp.stack(entering, axis=0), "seq", 0, 0, tiled=True)
    incoming = jnp.transpose(entering, (1, 0, 2, 3)).reshape(mamba_heads, HD, NS)
    carried = jnp.exp(cumulative)[:, :, None] * jnp.einsum(
        "tn,hpn->thp", c_mat, incoming, precision=high
    )
    mamba_y = inner_out + carried + d_skip[None, :, None] * x_conv
    state_after = block_decay[:, None, None] * incoming + own_state
    gated = mamba_y * jax.nn.silu(inner[:, 0].astype(jnp.float32).reshape(tokens, mamba_heads, HD))
    mixed = (
        rms_scale(gated).reshape(tokens, mamba_heads * HD) * mamba_gain.astype(jnp.float32)
    ).astype(jnp.bfloat16)
    cache_rows = cache.shape[1]
    shard_rows = cache_rows + tokens
    group = mp_pos * local_heads // (QH // KVH)
    query_index = seq_pos * tokens + jnp.arange(tokens, dtype=jnp.int32)
    scale = 1.0 / float(HD) ** 0.5
    piece = jnp.concatenate([cache_all, new_all], axis=0)
    top = jnp.full((local_heads, tokens), negative, jnp.float32)
    total_cache = cache_all.shape[0]
    index = jnp.arange(piece.shape[0], dtype=jnp.int32)
    in_cache = index < total_cache
    slot_ok = in_cache & (index < length)
    new_index = index - total_cache
    valid = slot_ok[None, :] | (~in_cache)[None, :] & (new_index[None, :] <= query_index[:, None])
    scores = (
        jnp.einsum("qhd,kd->hqk", query, piece[:, :HD], preferred_element_type=jnp.float32) * scale
    )
    masked = jnp.where(valid[None], scores, negative)
    new_top = jnp.maximum(top, jnp.max(masked, axis=-1))
    weights = jnp.where(valid[None], jnp.exp(masked - new_top[:, :, None]), 0.0)
    total = jnp.sum(weights, axis=-1)
    accum = jnp.einsum(
        "hqk,kd->hqd",
        weights.astype(jnp.bfloat16),
        piece[:, HD : 2 * HD],
        preferred_element_type=jnp.float32,
    )
    top, total, accum = (new_top, total, accum)
    attended = jnp.transpose(accum / total[:, :, None], (1, 0, 2)).reshape(tokens, local_heads * HD)
    attended = attended.astype(jnp.bfloat16)
    term = jnp.dot(attended, w_attn_out, preferred_element_type=jnp.float32)
    term = term + jnp.dot(mixed, w_mamba_out, preferred_element_type=jnp.float32)
    summed = lax.psum_scatter(term, "mp", scatter_dimension=1, tiled=True)
    layer = (summed + own_rows.astype(jnp.float32)).astype(jnp.bfloat16)
    return (layer[None], kv_block[None], state_after[None, None])


def solution(mesh):
    placed = (
        P("req", "seq", "mp"),
        P(),
        P(None, "mp"),
        P(None, "mp"),
        P("mp", None),
        P(None, None, "mp"),
        P(None, "mp"),
        P(None, "mp"),
        P("mp"),
        P("mp"),
        P("mp"),
        P(None, "mp"),
        P(),
        P("mp"),
        P("mp", None),
        P("req", "seq", "mp"),
        P("req"),
        P("req", None, "mp"),
        P("req", None, None),
        P("req", "mp", None, None),
    )
    return jax.shard_map(
        shards,
        mesh=mesh,
        in_specs=placed,
        out_specs=(P("req", "seq", "mp"), P("req", "seq", "mp"), P("req", "seq", "mp", None, None)),
        check_vma=False,
    )
```

profile of v0, /device:TPU:1, one launch (start us, length us, event | category | flops | bytes accessed | tf_op | source)
XLA Modules:
  0.0 330.6 jit_solution(8155268910153722102)
XLA Ops:
  8.9 2.1 collective-permute-start
  18.8 15.6 %and_or_fusion = pred[256,16384]{0,1:T(8,128)(4,1)} fusion(s32[256]{0:T(256)S(1)} %iota_add_fusion.1, s32[16384]{0:T(1024)S(1)} %iota_add_fusion, pred[16384]{0:T(1024)(128)(4,1)S(1)} %get-tuple-element.103, pred[16384]{0:T(1024)(128)(4,1)S(1)} %get-tuple-element.104), kind=kLoop, calls=%fused_computation.7 | loop fusion | flops 12582912 | bytes 4293632 | tf_op jit(solution)/shard_map/or | solution.py:185
  34.4 8.3 %all-gather.9.cloned.1.call-done = bf16[1,256,3072]{2,1,0:T(8,128)(2,1)} async-done(((bf16[1,256,768]{2,1,0:T(8,128)(2,1)}), bf16[1,256,3072]{2,1,0:T(8,128)(2,1)}) %all-gather.9.cloned.1.call-update) | async-done | bytes 1572880 | tf_op jit(solution)/shard_map/all_gather | solution.py:94
  42.7 1.8 fusion.9
  44.5 1.9 fusion.11
  49.5 4.3 %fusion.13 = bf16[256,2,384]{2,0,1:T(8,128)(2,1)S(1)} fusion(bf16[3072,2,384]{2,1,0:T(2,128)(2,1)} %param.25, bf16[256,3072]{1,0:T(8,128)(2,1)} %copy-done.1), kind=kOutput, calls=%fused_computation.20 | convolution fusion | flops 1208156160 | bytes 6684672 | tf_op jit(solution)/shard_map/td,dkc->tkc/dot_general | solution.py:125
  53.9 3.1 collective-permute-start.2
  58.6 9.8 %all_gather.15 = bf16[256,512]{1,0:T(8,128)(2,1)S(1)} all-gather(bf16[256,128]{1,0:T(8,128)(2,1)S(1)} %convolution_convert_fusion), channel_id=1, replica_groups=mesh['seq'=32,'mp'=4,'req'=2] {'mp'}, dimensions={1}, use_global_device_ids=true | all-gather | bytes 327680 | tf_op jit(solution)/shard_map/all_gather | solution.py:110
  68.4 2.7 collective-permute-start.3
  75.7 10.7 %all-to-all-start = ((f32[32,3,5,256]{3,1,2,0:T(4,128)}), f32[32,3,5,256]{3,1,2,0:T(4,128)}, u32[]{:S(2)}, u32[]{:S(2)}) async-start(f32[32,3,5,256]{3,1,2,0:T(4,128)} %pad_maximum_fusion), calls=%async_computation | async-start | bytes 1310720 | tf_op jit(solution)/shard_map/all_to_all | solution.py:155
  86.5 2.3 fusion.90
  90.8 1.5 collective-permute-done.1
  93.0 8.7 %all-to-all-done = f32[32,3,5,256]{3,1,2,0:T(4,128)} async-done(((f32[32,3,5,256]{3,1,2,0:T(4,128)}), f32[32,3,5,256]{3,1,2,0:T(4,128)}, u32[]{:S(2)}, u32[]{:S(2)}) %all-to-all-start) | async-done | bytes 491552 | tf_op jit(solution)/shard_map/all_to_all | solution.py:155
  122.8 1.9 copy.77
  124.7 7.0 %all-to-all-start.1 = ((f32[32,3,4,256]{3,2,1,0:T(4,128)}), f32[32,3,4,256]{3,2,1,0:T(4,128)}, u32[]{:S(2)}, u32[]{:S(2)}) async-start(f32[32,3,4,256]{3,2,1,0:T(4,128)} %copy.77), calls=%async_computation.1 | async-start | bytes 786432 | tf_op jit(solution)/shard_map/all_to_all | solution.py:162
  132.0 2.6 fusion.91
  136.3 1.9 copy.79
  138.2 1.7 copy.85
  140.0 1.8 subtract_convert_fusion
  143.6 1.8 copy.78
  145.3 1.9 reshape.277
  148.7 2.5 multiply_reduce_fusion
  151.4 4.6 %constant_dynamic-update-slice_fusion.1 = bf16[16384,256]{0,1:T(8,128)(2,1)} fusion(bf16[8192,256]{0,1:T(8,128)(2,1)} %all-gather.5.cloned.1.call-done), kind=kLoop, calls=%fused_computation.102 | loop fusion | bytes 8388608
  156.0 62.0 %all-gather.7.cloned.1.call-done = bf16[8192,256]{0,1:T(8,128)(2,1)} async-done(((bf16[256,256]{0,1:T(8,128)(2,1)}), bf16[8192,256]{0,1:T(8,128)(2,1)}) %all-gather.7.cloned.1.call-update) | async-done | bytes 4194320 | tf_op jit(solution)/shard_map/all_gather | solution.py:124
  218.0 4.6 %constant_dynamic-update-slice_fusion = bf16[16384,256]{0,1:T(8,128)(2,1)} fusion(bf16[16384,256]{0,1:T(8,128)(2,1)} %constant_dynamic-update-slice_fusion.1, bf16[8192,256]{0,1:T(8,128)(2,1)} %all-gather.7.cloned.1.call-done), kind=kLoop, calls=%fused_computation.101 | loop fusion | bytes 8388608 | tf_op jit(solution)/shard_map/concatenate | solution.py:178
  222.6 17.3 %fusion = (f32[2,256]{1,0:T(2,128)S(1)}, f32[16384,256,2]{1,0,2:T(8,128)}) fusion(pred[256,16384]{0,1:T(8,128)(4,1)} %and_or_fusion, bf16[256,2,64]{2,0,1:T(8,128)(2,1)S(1)} %copy-done.8, bf16[256,2,64]{2,0,1:T(8,128)(2,1)S(1)} %copy-done.7, bf16[16384,256]{0,1:T(8,128)(2,1)} %constant_dynamic-update-slice_fusion), kind=kOutput, calls=%fused_computation.2 | convolution fusion | flops 2172911104 | bytes 42076160 | tf_op jit(solution)/shard_map/qhd,kd->hqk/dot_general | solution.py:187
  239.9 15.7 %fusion.1 = f32[2,256]{1,0:T(2,128)S(1)} fusion(f32[16384,256,2]{1,0,2:T(8,128)} %get-tuple-element.98, f32[2,256]{1,0:T(2,128)S(1)} %broadcast_maximum_fusion, pred[256,16384]{0,1:T(8,128)(4,1)} %and_or_fusion), kind=kLoop, calls=%fused_computation.3 | loop fusion | flops 41942528 | bytes 37752832 | tf_op jit(solution)/shard_map/reduce_sum | solution.py:192
  255.6 17.2 %fusion.27 = bf16[256,2,128]{0,2,1:T(8,128)(2,1)S(1)} fusion(f32[16384,256,2]{1,0,2:T(8,128)} %get-tuple-element.98, f32[2,256]{1,0:T(2,128)S(1)} %broadcast_maximum_fusion, pred[256,16384]{0,1:T(8,128)(4,1)} %and_or_fusion, bf16[16384,256]{0,1:T(8,128)(2,1)} %constant_dynamic-update-slice_fusion, f32[256,2]{0,1:T(2,128)S(1)} %bitcast.367), kind=kOutput, calls=%fused_computation.30 | convolution fusion | flops 2189557760 | bytes 42078208 | tf_op jit(solution)/shard_map/hqk,kd->hqd/dot_general | solution.py:193
  272.8 2.0 fusion.92
  274.9 2.7 convolution_add_fusion
  279.2 42.8 %reduce-scatter.2.cloned.1.call-done = f32[256,768]{1,0:T(8,128)} async-done(((f32[256,3072]{1,0:T(8,128)}), f32[256,768]{1,0:T(8,128)}) %reduce-scatter.2.cloned.1.call-update) | async-done | bytes 786448 | tf_op jit(solution)/shard_map/reduce_scatter | solution.py:204
  322.0 2.0 fusion.40
  (151 shorter events, 48.6 us)
Async XLA Ops:
  7.2 267.7 %copy-start = (bf16[384,3072]{1,0:T(8,128)(2,1)S(1)}, bf16[384,3072]{1,0:T(8,128)(2,1)}, u32[]{:S(2)}) copy-start(bf16[384,3072]{1,0:T(8,128)(2,1)} %param.34) | copy-start | bytes 7077892
  7.2 35.5 %all-gather.9.cloned.1.call-start = ((), (), s32[]{:S(2)}) async-start(), calls=%async_computation.6 | async-start | bytes 1966080 | tf_op jit(solution)/shard_map/all_gather | solution.py:94
  7.9 143.5 %all-gather.5.cloned.1.call-start = ((), (), s32[]{:S(2)}) async-start(), calls=%async_computation.3 | async-start | bytes 4325376 | tf_op jit(solution)/shard_map/all_gather | solution.py:123
  8.9 9.2 %collective-permute-start = (bf16[256,128]{0,1:T(8,128)(2,1)S(1)}, bf16[256,128]{0,1:T(8,128)(2,1)S(1)}, u32[]{:S(2)}, u32[]{:S(2)}) collective-permute-start(bf16[256,128]{0,1:T(8,128)(2,1)S(1)} %bitcast.357), channel_id=1, source_target_pairs={{0,2},{2,0},{4,6},{6,4},{1,3},{3,1},{5,7},{7,5},{8,10},{10,8},{12,... | collective-permute-start | bytes 196616 | tf_op jit(solution)/shard_map/ppermute | solution.py:116
  18.8 28.8 %copy-start.9 = (bf16[3072,3]{0,1:T(4,128)(2,1)S(1)}, bf16[3072,3]{0,1:T(4,128)(2,1)}, u32[]{:S(2)}) copy-start(bf16[3072,3]{0,1:T(4,128)(2,1)} %param.27) | copy-start | bytes 55300
  18.8 28.8 %copy-start.14 = (f32[3]{0:T(128)S(1)}, f32[3]{0:T(128)}, u32[]{:S(2)}) copy-start(f32[3]{0:T(128)} %param.28) | copy-start | bytes 40
  46.4 1.2 copy-start.1
  49.5 8.6 %copy-start.2 = (bf16[256,3072]{1,0:T(8,128)(2,1)S(1)}, bf16[256,3072]{1,0:T(8,128)(2,1)}, u32[]{:S(2)}) copy-start(bf16[256,3072]{1,0:T(8,128)(2,1)} %copy-done.1) | copy-start | bytes 4718596
  49.5 8.6 %copy-start.4 = (bf16[3072,128]{1,0:T(8,128)(2,1)S(1)}, bf16[3072,128]{1,0:T(8,128)(2,1)}, u32[]{:S(2)}) copy-start(bf16[3072,128]{1,0:T(8,128)(2,1)} %param.26) | copy-start | bytes 2359300
  49.5 21.7 %copy-start.11 = (bf16[1,3,384]{2,1,0:T(4,128)(2,1)S(1)}, bf16[1,3,384]{2,1,0:T(4,128)(2,1)}, u32[]{:S(2)}) copy-start(bf16[1,3,384]{2,1,0:T(4,128)(2,1)} %param.37) | copy-start | bytes 6916
  53.8 18.6 %copy-start.10 = (bf16[1,3,512]{2,1,0:T(4,128)(2,1)S(1)}, bf16[1,3,512]{2,1,0:T(4,128)(2,1)}, u32[]{:S(2)}) copy-start(bf16[1,3,512]{2,1,0:T(4,128)(2,1)} %param.38) | copy-start | bytes 9220
  53.9 17.3 %collective-permute-start.2 = (bf16[3,384]{1,0:T(4,128)(2,1)S(1)}, bf16[3,384]{1,0:T(4,128)(2,1)S(1)}, u32[]{:S(2)}, u32[]{:S(2)}) collective-permute-start(bf16[3,384]{1,0:T(4,128)(2,1)S(1)} %slice_bitcast_fusion.73), channel_id=1, source_target_pairs={{0,8},{8,16},{16,24},{24,32},{32,40},{40,48},{48,56},{56,64},{64,7... | collective-permute-start | bytes 6920 | tf_op jit(solution)/shard_map/ppermute | solution.py:19
  68.4 6.2 %copy-start.12 = (f32[3]{0:T(128)}, f32[3]{0:T(128)S(1)}, u32[]{:S(2)}) copy-start(f32[3]{0:T(128)S(1)} %exp.54) | copy-start | bytes 40
  68.4 4.0 %collective-permute-start.3 = (bf16[3,512]{1,0:T(4,128)(2,1)S(1)}, bf16[3,512]{1,0:T(4,128)(2,1)S(1)}, u32[]{:S(2)}, u32[]{:S(2)}) collective-permute-start(bf16[3,512]{1,0:T(4,128)(2,1)S(1)} %slice.510), channel_id=1, source_target_pairs={{0,8},{8,16},{16,24},{24,32},{32,40},{40,48},{48,56},{56,64},{64,7... | collective-permute-start | bytes 9224 | tf_op jit(solution)/shard_map/ppermute | solution.py:19
  75.7 26.1 %all-to-all-start = ((f32[32,3,5,256]{3,1,2,0:T(4,128)}), f32[32,3,5,256]{3,1,2,0:T(4,128)}, u32[]{:S(2)}, u32[]{:S(2)}) async-start(f32[32,3,5,256]{3,1,2,0:T(4,128)} %pad_maximum_fusion), calls=%async_computation | async-start | bytes 1310720 | tf_op jit(solution)/shard_map/all_to_all | solution.py:155
  86.4 131.6 %all-gather.7.cloned.1.call-start = ((), (), s32[]{:S(2)}) async-start(), calls=%async_computation.4 | async-start | bytes 4325376 | tf_op jit(solution)/shard_map/all_gather | solution.py:124
  89.1 3.2 copy-start.5
  89.1 3.2 collective-permute-start.1
  124.7 18.9 %all-to-all-start.1 = ((f32[32,3,4,256]{3,2,1,0:T(4,128)}), f32[32,3,4,256]{3,2,1,0:T(4,128)}, u32[]{:S(2)}, u32[]{:S(2)}) async-start(f32[32,3,4,256]{3,2,1,0:T(4,128)} %copy.77), calls=%async_computation.1 | async-start | bytes 786432 | tf_op jit(solution)/shard_map/all_to_all | solution.py:162
  131.7 190.3 %reduce-scatter.2.cloned.1.call-start = ((), (), s32[]{:S(2)}) async-start(), calls=%async_computation.5 | async-start | bytes 3932160 | tf_op jit(solution)/shard_map/reduce_scatter | solution.py:204
  156.0 66.6 %copy-start.7 = (bf16[256,2,64]{2,0,1:T(8,128)(2,1)S(1)}, bf16[256,2,64]{2,0,1:T(8,128)(2,1)}, u32[]{:S(2)}) copy-start(bf16[256,2,64]{2,0,1:T(8,128)(2,1)} %get-tuple-element.49) | copy-start | bytes 196612
  156.0 66.6 %copy-start.8 = (bf16[256,2,64]{2,0,1:T(8,128)(2,1)S(1)}, bf16[256,2,64]{2,0,1:T(8,128)(2,1)}, u32[]{:S(2)}) copy-start(bf16[256,2,64]{2,0,1:T(8,128)(2,1)} %get-tuple-element.50) | copy-start | bytes 196612
  274.9 2.8 copy-start.6
  274.9 3.5 %copy-start.3 = (f32[3,128,256]{2,1,0:T(8,128)S(1)}, f32[3,128,256]{2,1,0:T(8,128)}, u32[]{:S(2)}) copy-start(f32[3,128,256]{2,1,0:T(8,128)} %reshape.277) | copy-start | bytes 1179652
  274.9 3.5 %copy-start.13 = (f32[3]{0:T(128)S(1)}, f32[3]{0:T(128)}, u32[]{:S(2)}) copy-start(f32[3]{0:T(128)} %copy-done.12) | copy-start | bytes 40
Sparse Core Ops, SparseCore 0:
  9.8 32.8 all-gather.8
  45.2 86.1 all-gather.4
  133.8 84.1 all-gather.6
  277.7 44.2 reduce-scatter.1
where the time goes:
time: 332 us; the launch traced here: 331 us
  waiting for transfers between devices  125 us (38%)
  other arithmetic  69.1 us (21%)
  matrix products  55.4 us (17%)
  local copies, waits for them, and re-layouts  28.8 us (9%)
  starting transfers between devices  27.1 us (8%)
  between operations  14.9 us (4%)
  blocking collectives  9.8 us (3%)
    all_gather x1, waiting for transfers between devices, shards(): new_all = lax.all_gather(paired(kv_block), 'seq', axis=0, tiled=True)  62 us
    reduce_scatter x1, waiting for transfers between devices, shards(): summed = lax.psum_scatter(term, 'mp', scatter_dimension=1, tiled=True)  42.8 us
    unnamed x31, other arithmetic  18.3 us
    dot_general x1, matrix products, shards(): jnp.einsum('qhd,kd->hqk', query, piece[:, :HD], preferred_element_type=jn...  17.3 us
    dot_general x1, matrix products, shards(): jnp.einsum('hqk,kd->hqd', weights.astype(jnp.bfloat16), piece[:, HD:2 * H...  17.2 us
    reduce_sum x1, other arithmetic, shards(): total = jnp.sum(weights, axis=-1)  15.7 us
    or x1, other arithmetic, shards(): slot_ok[None, :]  15.6 us
    unnamed x37, local copies, waits for them, and re-layouts  10.8 us
  transfers between devices with their start and end apart: 10, of which 6 were waited for; matrix products, arithmetic and copies ran while one was open for 27% of the time, Pallas kernels for 0%

commit v1 on v0

--- a/solution.py
+++ b/solution.py
@@ -91,7 +91,23 @@
     seq_pos = lax.axis_index("seq")
     mp_pos = lax.axis_index("mp")
     length = cache_len[0]
-    whole = lax.all_gather(own_rows, "mp", axis=1, tiled=True)
+    peers, mine, span = (lax.axis_size("mp"), lax.axis_index("mp"), own_rows.shape[1])
+    right = [(i_2, (i_2 + 1) % peers) for i_2 in range(peers)]
+    downward = [(i_2, (i_2 - 1) % peers) for i_2 in range(peers)]
+    whole = jnp.zeros((*own_rows.shape[:1], peers * span, *own_rows.shape[1 + 1 :]), own_rows.dtype)
+    whole = lax.dynamic_update_slice_in_dim(whole, own_rows, mine * span, axis=1)
+    from_left = from_right = own_rows
+    middle = peers // 2
+    for step in range(1, middle + 1):
+        from_left = lax.ppermute(from_left, "mp", right)
+        whole = lax.dynamic_update_slice_in_dim(
+            whole, from_left, (mine - step) % peers * span, axis=1
+        )
+        if step < peers - middle:
+            from_right = lax.ppermute(from_right, "mp", downward)
+            whole = lax.dynamic_update_slice_in_dim(
+                whole, from_right, (mine + step) % peers * span, axis=1
+            )
     normed = (rms_scale(whole.astype(jnp.float32)) * norm_gain.astype(jnp.float32)).astype(
         jnp.bfloat16
     )

time: 332 us -> 317 us (0.955)
  waiting for transfers between devices: 125 us -> 85.6 us
  other arithmetic: 69.1 us -> 81.6 us
  local copies, waits for them, and re-layouts: 28.8 us -> 34.7 us
  starting transfers between devices: 27.1 us -> 32.5 us
    all_gather x1, waiting for transfers between devices: 62 us -> 24.1 us  [shards(): new_all = lax.all_gather(paired(kv_block), 'seq', axis=0, tiled=True)]
    all_gather x1 -> x0, waiting for transfers between devices: 8.26 us -> none  [shards(): whole = lax.all_gather(own_rows, 'mp', axis=1, tiled=True)]
    or x1, other arithmetic: 15.6 us -> 22.6 us  [shards(): slot_ok[None, :]]
    ppermute x2, waiting for transfers between devices: 1.52 us -> 7.87 us  [paired(): other = lax.ppermute(own, 'mp', pairs_of)]
    ppermute x0 -> x3, starting transfers between devices: none -> 3.86 us  [the longest x2 2.5 us: shards(): from_left = lax.ppermute(from_left, 'mp', right)]
    unnamed x37 -> x73, local copies, waits for them, and re-layouts: 10.8 us -> 11.6 us
  transfers between devices with their start and end apart: 10 -> 12, of which waited for: 6 -> 7; matrix products, arithmetic and copies ran while one was open for 27% -> 35% of each run, Pallas kernels for 0% -> 0%
where the time goes in v1:
time: 317 us; the launch traced here: 316 us
  waiting for transfers between devices  85.6 us (27%)
  other arithmetic  81.6 us (26%)
  matrix products  55.7 us (18%)
  local copies, waits for them, and re-layouts  34.7 us (11%)
  starting transfers between devices  32.5 us (10%)
  between operations  15.2 us (5%)
  blocking collectives  10.3 us (3%)
    reduce_scatter x1, waiting for transfers between devices, shards(): summed = lax.psum_scatter(term, 'mp', scatter_dimension=1, tiled=True)  42.8 us
    all_gather x1, waiting for transfers between devices, shards(): new_all = lax.all_gather(paired(kv_block), 'seq', axis=0, tiled=True)  24.1 us
    or x1, other arithmetic, shards(): slot_ok[None, :]  22.6 us
    unnamed x31, other arithmetic  18.3 us
    dot_general x1, matrix products, shards(): jnp.einsum('qhd,kd->hqk', query, piece[:, :HD], preferred_element_type=jn...  17.5 us
    dot_general x1, matrix products, shards(): jnp.einsum('hqk,kd->hqd', weights.astype(jnp.bfloat16), piece[:, HD:2 * H...  17.2 us
    reduce_sum x1, other arithmetic, shards(): total = jnp.sum(weights, axis=-1)  15.6 us
    all_to_all x1, starting transfers between devices, shards(): lax.all_to_all(jnp.concatenate([pieces, decays], axis=2), 'seq', 0, 0, ti...  12.7 us
  transfers between devices with their start and end apart: 12, of which 7 were waited for; matrix products, arithmetic and copies ran while one was open for 35% of the time, Pallas kernels for 0%

profile of v1, /device:TPU:1, one launch (start us, length us, event | category | flops | bytes accessed | tf_op | source)
XLA Modules:
  0.0 315.6 jit_solution(10771457005133139884)
XLA Ops:
  7.2 2.1 collective-permute-start.1
  14.9 5.4 %collective-permute-done = bf16[256,128]{0,1:T(8,128)(2,1)} collective-permute-done((bf16[256,128]{0,1:T(8,128)(2,1)}, bf16[256,128]{0,1:T(8,128)(2,1)}, u32[]{:S(2)}, u32[]{:S(2)}) %collective-permute-start) | collective-permute-done | bytes 65568 | tf_op jit(solution)/shard_map/ppermute | solution.py:132
  21.9 22.6 %and_or_fusion = pred[256,16384]{0,1:T(8,128)(4,1)} fusion(s32[256]{0:T(256)} %iota_add_fusion.1, s32[16384]{0:T(1024)} %iota_add_fusion, pred[16384]{0:T(1024)(128)(4,1)S(1)} %get-tuple-element.103, pred[16384]{0:T(1024)(128)(4,1)} %get-tuple-element.104), kind=kLoop, calls=%fused_computation.7 | loop fusion | flops 12582912 | bytes 4293632 | tf_op jit(solution)/shard_map/or | solution.py:201
  59.7 1.8 fusion.9
  61.5 1.9 fusion.11
  66.5 4.3 %fusion.13 = bf16[256,2,384]{2,0,1:T(8,128)(2,1)S(1)} fusion(bf16[3072,2,384]{2,1,0:T(2,128)(2,1)} %param.25, bf16[256,3072]{1,0:T(8,128)(2,1)} %copy-done.1), kind=kOutput, calls=%fused_computation.20 | convolution fusion | flops 1208156160 | bytes 6684672 | tf_op jit(solution)/shard_map/td,dkc->tkc/dot_general | solution.py:141
  70.9 3.9 %collective-permute-start.5 = (bf16[3,384]{1,0:T(4,128)(2,1)S(1)}, bf16[3,384]{1,0:T(4,128)(2,1)S(1)}, u32[]{:S(2)}, u32[]{:S(2)}) collective-permute-start(bf16[3,384]{1,0:T(4,128)(2,1)S(1)} %slice_bitcast_fusion.73), channel_id=1, source_target_pairs={{0,8},{8,16},{16,24},{24,32},{32,40},{40,48},{48,56},{56,64},{64,7... | collective-permute-start | bytes 6920 | tf_op jit(solution)/shard_map/ppermute | solution.py:19
  77.0 10.3 %all_gather.11 = bf16[256,512]{1,0:T(8,128)(2,1)S(1)} all-gather(bf16[256,128]{1,0:T(8,128)(2,1)S(1)} %convolution_convert_fusion), channel_id=1, replica_groups=mesh['seq'=32,'mp'=4,'req'=2] {'mp'}, dimensions={1}, use_global_device_ids=true | all-gather | bytes 327680 | tf_op jit(solution)/shard_map/all_gather | solution.py:126
  87.3 2.5 collective-permute-start.6
  94.5 12.7 %all-to-all-start = ((f32[32,3,5,256]{3,1,2,0:T(4,128)}), f32[32,3,5,256]{3,1,2,0:T(4,128)}, u32[]{:S(2)}, u32[]{:S(2)}) async-start(f32[32,3,5,256]{3,1,2,0:T(4,128)} %pad_maximum_fusion), calls=%async_computation | async-start | bytes 1310720 | tf_op jit(solution)/shard_map/all_to_all | solution.py:171
  107.3 2.3 fusion.89
  110.9 2.4 collective-permute-done.4
  114.1 8.0 %all-to-all-done = f32[32,3,5,256]{3,1,2,0:T(4,128)} async-done(((f32[32,3,5,256]{3,1,2,0:T(4,128)}), f32[32,3,5,256]{3,1,2,0:T(4,128)}, u32[]{:S(2)}, u32[]{:S(2)}) %all-to-all-start) | async-done | bytes 491552 | tf_op jit(solution)/shard_map/all_to_all | solution.py:171
  143.0 1.9 copy.77
  144.9 9.1 %all-to-all-start.1 = ((f32[32,3,4,256]{3,2,1,0:T(4,128)}), f32[32,3,4,256]{3,2,1,0:T(4,128)}, u32[]{:S(2)}, u32[]{:S(2)}) async-start(f32[32,3,4,256]{3,2,1,0:T(4,128)} %copy.77), calls=%async_computation.1 | async-start | bytes 786432 | tf_op jit(solution)/shard_map/all_to_all | solution.py:178
  154.1 2.6 fusion.90
  158.4 1.9 copy.79
  162.1 1.8 subtract_convert_fusion
  164.3 1.9 all-to-all-done.1
  166.3 1.8 copy.78
  168.0 1.9 reshape.277
  171.4 2.6 multiply_reduce_fusion
  174.2 4.6 %constant_dynamic-update-slice_fusion.1 = bf16[16384,256]{0,1:T(8,128)(2,1)} fusion(bf16[8192,256]{0,1:T(8,128)(2,1)} %all-gather.3.cloned.1.call-done), kind=kLoop, calls=%fused_computation.101 | loop fusion | bytes 8388608
  178.8 24.1 %all-gather.5.cloned.1.call-done = bf16[8192,256]{0,1:T(8,128)(2,1)} async-done(((bf16[256,256]{0,1:T(8,128)(2,1)}), bf16[8192,256]{0,1:T(8,128)(2,1)}) %all-gather.5.cloned.1.call-update) | async-done | bytes 4194320 | tf_op jit(solution)/shard_map/all_gather | solution.py:140
  202.9 4.6 %constant_dynamic-update-slice_fusion = bf16[16384,256]{0,1:T(8,128)(2,1)} fusion(bf16[16384,256]{0,1:T(8,128)(2,1)} %constant_dynamic-update-slice_fusion.1, bf16[8192,256]{0,1:T(8,128)(2,1)} %all-gather.5.cloned.1.call-done), kind=kLoop, calls=%fused_computation.100 | loop fusion | bytes 8388608 | tf_op jit(solution)/shard_map/concatenate | solution.py:194
  207.5 17.5 %fusion = (f32[2,256]{1,0:T(2,128)S(1)}, f32[16384,256,2]{1,0,2:T(8,128)}) fusion(pred[256,16384]{0,1:T(8,128)(4,1)} %and_or_fusion, bf16[256,2,64]{2,0,1:T(8,128)(2,1)S(1)} %copy-done.9, bf16[256,2,64]{2,0,1:T(8,128)(2,1)S(1)} %copy-done.8, bf16[16384,256]{0,1:T(8,128)(2,1)} %constant_dynamic-update-slice_fusion), kind=kOutput, calls=%fused_computation.2 | convolution fusion | flops 2172911104 | bytes 42076160 | tf_op jit(solution)/shard_map/qhd,kd->hqk/dot_general | solution.py:203
  225.0 15.6 %fusion.1 = f32[2,256]{1,0:T(2,128)S(1)} fusion(f32[16384,256,2]{1,0,2:T(8,128)} %get-tuple-element.98, f32[2,256]{1,0:T(2,128)S(1)} %broadcast_maximum_fusion, pred[256,16384]{0,1:T(8,128)(4,1)} %and_or_fusion), kind=kLoop, calls=%fused_computation.3 | loop fusion | flops 41942528 | bytes 37752832 | tf_op jit(solution)/shard_map/reduce_sum | solution.py:208
  240.6 17.2 %fusion.27 = bf16[256,2,128]{0,2,1:T(8,128)(2,1)S(1)} fusion(f32[16384,256,2]{1,0,2:T(8,128)} %get-tuple-element.98, f32[2,256]{1,0:T(2,128)S(1)} %broadcast_maximum_fusion, pred[256,16384]{0,1:T(8,128)(4,1)} %and_or_fusion, bf16[16384,256]{0,1:T(8,128)(2,1)} %constant_dynamic-update-slice_fusion, f32[256,2]{0,1:T(2,128)S(1)} %bitcast.365), kind=kOutput, calls=%fused_computation.30 | convolution fusion | flops 2189557760 | bytes 42078208 | tf_op jit(solution)/shard_map/hqk,kd->hqd/dot_general | solution.py:209
  257.9 2.0 fusion.91
  259.9 2.7 convolution_add_fusion
  264.2 42.8 %reduce-scatter.2.cloned.1.call-done = f32[256,768]{1,0:T(8,128)} async-done(((f32[256,3072]{1,0:T(8,128)}), f32[256,768]{1,0:T(8,128)}) %reduce-scatter.2.cloned.1.call-update) | async-done | bytes 786448 | tf_op jit(solution)/shard_map/reduce_scatter | solution.py:220
  307.0 2.0 fusion.39
  (195 shorter events, 61.5 us)
Async XLA Ops:
  7.2 252.7 %copy-start = (bf16[384,3072]{1,0:T(8,128)(2,1)S(1)}, bf16[384,3072]{1,0:T(8,128)(2,1)}, u32[]{:S(2)}) copy-start(bf16[384,3072]{1,0:T(8,128)(2,1)} %param.34) | copy-start | bytes 7077892
  7.2 41.4 %copy-start.4 = (bf16[1,256,768]{2,1,0:T(8,128)(2,1)S(1)}, bf16[1,256,768]{2,1,0:T(8,128)(2,1)}, u32[]{:S(2)}) copy-start(bf16[1,256,768]{2,1,0:T(8,128)(2,1)} %param.20) | copy-start | bytes 1179652
  7.2 167.0 %all-gather.3.cloned.1.call-start = ((), (), s32[]{:S(2)}) async-start(), calls=%async_computation.3 | async-start | bytes 4325376 | tf_op jit(solution)/shard_map/all_gather | solution.py:139
  7.2 42.1 %collective-permute-start.1 = (bf16[256,768]{1,0:T(8,128)(2,1)}, bf16[256,768]{1,0:T(8,128)(2,1)S(1)}, u32[]{:S(2)}, u32[]{:S(2)}) collective-permute-start(bf16[256,768]{1,0:T(8,128)(2,1)} %bitcast.349), channel_id=1, source_target_pairs={{0,2},{2,4},{4,6},{6,0},{1,3},{3,5},{5,7},{7,1},{8,10},{10,12},{12... | collective-permute-start | bytes 1179656 | tf_op jit(solution)/shard_map/ppermute | solution.py:102
  9.4 47.8 %collective-permute-start.2 = (bf16[256,768]{1,0:T(8,128)(2,1)}, bf16[256,768]{1,0:T(8,128)(2,1)S(1)}, u32[]{:S(2)}, u32[]{:S(2)}) collective-permute-start(bf16[256,768]{1,0:T(8,128)(2,1)} %bitcast.350), channel_id=1, source_target_pairs={{0,6},{2,0},{4,2},{6,4},{1,7},{3,1},{5,3},{7,5},{8,14},{10,8},{12,... | collective-permute-start | bytes 1179656 | tf_op jit(solution)/shard_map/ppermute | solution.py:107
  12.3 8.0 %collective-permute-start = (bf16[256,128]{0,1:T(8,128)(2,1)}, bf16[256,128]{0,1:T(8,128)(2,1)}, u32[]{:S(2)}, u32[]{:S(2)}) collective-permute-start(bf16[256,128]{0,1:T(8,128)(2,1)} %bitcast.355), channel_id=1, source_target_pairs={{0,2},{2,0},{4,6},{6,4},{1,3},{3,1},{5,7},{7,5},{8,10},{10,8},{12,... | collective-permute-start | bytes 196616 | tf_op jit(solution)/shard_map/ppermute | solution.py:132
  48.6 16.0 %copy-start.31 = (f32[3]{0:T(128)S(1)}, f32[3]{0:T(128)}, u32[]{:S(2)}) copy-start(f32[3]{0:T(128)} %param.28) | copy-start | bytes 40
  49.4 9.5 %collective-permute-start.3 = (bf16[256,768]{1,0:T(8,128)(2,1)S(1)}, bf16[256,768]{1,0:T(8,128)(2,1)S(1)}, u32[]{:S(2)}, u32[]{:S(2)}) collective-permute-start(bf16[256,768]{1,0:T(8,128)(2,1)S(1)} %collective-permute-done.1), channel_id=1, source_target_pairs={{0,2},{2,4},{4,6},{6,0},{1,3},{3,5},{5,7},{7,1},{8,10},{10,12},{12... | collective-permute-start | bytes 1179656 | tf_op jit(solution)/shard_map/ppermute | solution.py:102
  66.4 23.4 %copy-start.26 = (bf16[1,3,384]{2,1,0:T(4,128)(2,1)S(1)}, bf16[1,3,384]{2,1,0:T(4,128)(2,1)}, u32[]{:S(2)}) copy-start(bf16[1,3,384]{2,1,0:T(4,128)(2,1)} %param.37) | copy-start | bytes 6916
  70.8 19.1 %copy-start.18 = (f32[384]{0:T(512)S(1)}, f32[384]{0:T(512)}, u32[]{:S(2)}) copy-start(f32[384]{0:T(512)} %get-tuple-element.15) | copy-start | bytes 4612
  70.8 19.1 %copy-start.19 = (f32[384]{0:T(512)S(1)}, f32[384]{0:T(512)}, u32[]{:S(2)}) copy-start(f32[384]{0:T(512)} %get-tuple-element.16) | copy-start | bytes 4612
  70.8 19.1 %copy-start.20 = (f32[384]{0:T(512)S(1)}, f32[384]{0:T(512)}, u32[]{:S(2)}) copy-start(f32[384]{0:T(512)} %get-tuple-element.17) | copy-start | bytes 4612
  70.8 19.1 %copy-start.21 = (f32[384]{0:T(512)S(1)}, f32[384]{0:T(512)}, u32[]{:S(2)}) copy-start(f32[384]{0:T(512)} %get-tuple-element.18) | copy-start | bytes 4612
  70.9 20.3 %copy-start.24 = (bf16[1,3,512]{2,1,0:T(4,128)(2,1)S(1)}, bf16[1,3,512]{2,1,0:T(4,128)(2,1)}, u32[]{:S(2)}) copy-start(bf16[1,3,512]{2,1,0:T(4,128)(2,1)} %param.38) | copy-start | bytes 9220
  70.9 20.4 %copy-start.14 = (f32[1,512]{1,0:T(1,128)S(1)}, f32[1,512]{1,0:T(1,128)}, u32[]{:S(2)}) copy-start(f32[1,512]{1,0:T(1,128)} %get-tuple-element.90) | copy-start | bytes 6148
  70.9 20.4 %copy-start.15 = (f32[1,512]{1,0:T(1,128)S(1)}, f32[1,512]{1,0:T(1,128)}, u32[]{:S(2)}) copy-start(f32[1,512]{1,0:T(1,128)} %get-tuple-element.91) | copy-start | bytes 6148
  70.9 20.4 %copy-start.16 = (f32[1,512]{1,0:T(1,128)S(1)}, f32[1,512]{1,0:T(1,128)}, u32[]{:S(2)}) copy-start(f32[1,512]{1,0:T(1,128)} %get-tuple-element.92) | copy-start | bytes 6148
  70.9 20.4 %copy-start.17 = (f32[1,512]{1,0:T(1,128)S(1)}, f32[1,512]{1,0:T(1,128)}, u32[]{:S(2)}) copy-start(f32[1,512]{1,0:T(1,128)} %get-tuple-element.93) | copy-start | bytes 6148
  70.9 18.9 %collective-permute-start.5 = (bf16[3,384]{1,0:T(4,128)(2,1)S(1)}, bf16[3,384]{1,0:T(4,128)(2,1)S(1)}, u32[]{:S(2)}, u32[]{:S(2)}) collective-permute-start(bf16[3,384]{1,0:T(4,128)(2,1)S(1)} %slice_bitcast_fusion.73), channel_id=1, source_target_pairs={{0,8},{8,16},{16,24},{24,32},{32,40},{40,48},{48,56},{56,64},{64,7... | collective-permute-start | bytes 6920 | tf_op jit(solution)/shard_map/ppermute | solution.py:19
  87.3 3.8 %collective-permute-start.6 = (bf16[3,512]{1,0:T(4,128)(2,1)S(1)}, bf16[3,512]{1,0:T(4,128)(2,1)S(1)}, u32[]{:S(2)}, u32[]{:S(2)}) collective-permute-start(bf16[3,512]{1,0:T(4,128)(2,1)S(1)} %slice.510), channel_id=1, source_target_pairs={{0,8},{8,16},{16,24},{24,32},{32,40},{40,48},{48,56},{56,64},{64,7... | collective-permute-start | bytes 9224 | tf_op jit(solution)/shard_map/ppermute | solution.py:19
  91.6 17.9 %copy-start.23 = (f32[256]{0:T(256)S(1)}, f32[256]{0:T(256)}, u32[]{:S(2)}) copy-start(f32[256]{0:T(256)} %copy-done.22) | copy-start | bytes 3076
  91.6 17.9 %copy-start.30 = (f32[64]{0:T(128)S(1)}, f32[64]{0:T(128)}, u32[]{:S(2)}) copy-start(f32[64]{0:T(128)} %copy-done.29) | copy-start | bytes 772
  94.5 27.5 %all-to-all-start = ((f32[32,3,5,256]{3,1,2,0:T(4,128)}), f32[32,3,5,256]{3,1,2,0:T(4,128)}, u32[]{:S(2)}, u32[]{:S(2)}) async-start(f32[32,3,5,256]{3,1,2,0:T(4,128)} %pad_maximum_fusion), calls=%async_computation | async-start | bytes 1310720 | tf_op jit(solution)/shard_map/all_to_all | solution.py:171
  107.3 95.6 %all-gather.5.cloned.1.call-start = ((), (), s32[]{:S(2)}) async-start(), calls=%async_computation.4 | async-start | bytes 4325376 | tf_op jit(solution)/shard_map/all_gather | solution.py:140
  110.0 3.4 %collective-permute-start.4 = (bf16[256,128]{0,1:T(8,128)(2,1)S(1)}, bf16[256,128]{0,1:T(8,128)(2,1)S(1)}, u32[]{:S(2)}, u32[]{:S(2)}) collective-permute-start(bf16[256,128]{0,1:T(8,128)(2,1)S(1)} %fusion.61), channel_id=1, source_target_pairs={{0,2},{2,0},{4,6},{6,4},{1,3},{3,1},{5,7},{7,5},{8,10},{10,8},{12,... | collective-permute-start | bytes 196616 | tf_op jit(solution)/shard_map/ppermute | solution.py:132
  144.9 21.3 %all-to-all-start.1 = ((f32[32,3,4,256]{3,2,1,0:T(4,128)}), f32[32,3,4,256]{3,2,1,0:T(4,128)}, u32[]{:S(2)}, u32[]{:S(2)}) async-start(f32[32,3,4,256]{3,2,1,0:T(4,128)} %copy.77), calls=%async_computation.1 | async-start | bytes 786432 | tf_op jit(solution)/shard_map/all_to_all | solution.py:178
  154.0 17.4 %copy-start.12 = (f32[1,3,2,128]{3,1,2,0:T(4,128)S(1)}, f32[1,3,2,128]{3,1,2,0:T(4,128)}, u32[]{:S(2)}) copy-start(f32[1,3,2,128]{3,1,2,0:T(4,128)} %copy-done.11) | copy-start | bytes 9220
  154.0 17.4 %copy-start.25 = (f32[256,3]{0,1:T(4,128)S(1)}, f32[256,3]{0,1:T(4,128)}, u32[]{:S(2)}) copy-start(f32[256,3]{0,1:T(4,128)} %get-tuple-element.88) | copy-start | bytes 9220
  154.0 153.0 %reduce-scatter.2.cloned.1.call-start = ((), (), s32[]{:S(2)}) async-start(), calls=%async_computation.5 | async-start | bytes 3932160 | tf_op jit(solution)/shard_map/reduce_scatter | solution.py:220
  163.9 10.2 %copy-start.13 = (f32[384]{0:T(512)S(1)}, f32[384]{0:T(512)}, u32[]{:S(2)}) copy-start(f32[384]{0:T(512)} %convert_element_type.91) | copy-start | bytes 4612
  178.8 28.7 %copy-start.8 = (bf16[256,2,64]{2,0,1:T(8,128)(2,1)S(1)}, bf16[256,2,64]{2,0,1:T(8,128)(2,1)}, u32[]{:S(2)}) copy-start(bf16[256,2,64]{2,0,1:T(8,128)(2,1)} %get-tuple-element.49) | copy-start | bytes 196612
  178.8 28.7 %copy-start.9 = (bf16[256,2,64]{2,0,1:T(8,128)(2,1)S(1)}, bf16[256,2,64]{2,0,1:T(8,128)(2,1)}, u32[]{:S(2)}) copy-start(bf16[256,2,64]{2,0,1:T(8,128)(2,1)} %get-tuple-element.50) | copy-start | bytes 196612
  (13 other events, 70.8 us)
Sparse Core Ops, SparseCore 0:
  22.1 84.3 all-gather.2
  114.2 88.6 all-gather.4
  262.8 44.2 reduce-scatter.1
